TPU v7x, 256 devices: a whole 4x4x8 slice. The times are simulated.
256 devices in a mesh: tile: 32 (over y_hi, z, core), seg: 8 (over x, y_lo).
Axes of the slice: x: 4, y: 4 (y_hi: 2, y_lo: 2; y = y_hi * 2 + y_lo), z: 8, core: 2. Of those that a mesh axis runs over, the one named last changes fastest.
Arguments:
- right_sides: float32 [524288, 512], P(('tile', 'seg')), may hold values from -6 to 6
- leaf_proj: float32 [32, 128, 64, 128], P('tile', 'seg'), may hold values from -0.5 to 0.5
- col_levels: float32 [32, 4, 64, 128, 128], P('tile', None, 'seg'), may hold values from -0.5 to 0.5
- middle_factor: float32 [32, 128, 64, 64], P('tile', 'seg'), may hold values from -0.75 to 0.75
- row_levels: float32 [32, 4, 64, 128, 128], P('tile', None, 'seg'), may hold values from -0.5 to 0.5
- leaf_expand: float32 [32, 128, 128, 64], P('tile', 'seg'), may hold values from -0.125 to 0.125
Outputs:
- product: float32 [16384, 512], P(('seg', 'tile'))
All inputs are finite; a program needn't handle non-finite values.
Results may differ from a plain program's by a relative error of at most 0.0001.
Values sent between devices are 32-bit elements; how exact they have to be, the bound alone decides.
A program may use at most 64 MiB of HBM per device.

v0:
```python
import jax
import jax.numpy as jnp
from jax import lax
from jax.sharding import PartitionSpec as P

K = 64
LEAF = 128
LVL = 4
BOX = 16


def levels(coeffs, weights):
    width = coeffs.shape[-1]
    for level in range(LVL):
        stride = 2**level
        blocks = BOX // (2 * stride)
        wide = weights[level].reshape(blocks, stride, 2, K, 2, K)
        split = coeffs.reshape(blocks, 2, stride, K, width)
        mixed = jnp.einsum("aeuvwx,awexr->auevr", wide, split, precision=lax.Precision.HIGHEST)
        coeffs = mixed.reshape(BOX, K, width)
    return coeffs


def tile_product(columns, leaf_proj, col_levels, middle_factor, row_levels, leaf_expand):
    width = columns.shape[1]
    coeffs = jnp.einsum(
        "nkl,nlr->nkr",
        leaf_proj[0],
        columns.reshape(BOX, LEAF, width),
        precision=lax.Precision.HIGHEST,
    )
    coeffs = levels(coeffs, col_levels[0])
    coeffs = jnp.einsum("nkj,njr->nkr", middle_factor[0], coeffs, precision=lax.Precision.HIGHEST)
    coeffs = lax.all_to_all(coeffs, "seg", split_axis=0, concat_axis=0, tiled=True)
    coeffs = levels(coeffs, row_levels[0])
    expand = leaf_expand[0]
    out_rows = BOX * LEAF // lax.axis_size("tile")
    leaf_count = min(BOX, lax.axis_size("tile") * out_rows // LEAF + 2)
    rows = jnp.einsum("nlk,nkr->nlr", expand, coeffs, precision=lax.Precision.HIGHEST)
    rows = rows.reshape(leaf_count * LEAF, width)
    return lax.psum_scatter(rows, "tile", scatter_dimension=0, tiled=True)


def shards(right_sides, leaf_proj, col_levels, middle_factor, row_levels, leaf_expand):
    return tile_product(right_sides, leaf_proj, col_levels, middle_factor, row_levels, leaf_expand)


def solution(mesh):
    in_specs = (
        P(("tile", "seg"), None),
        P("tile", "seg", None, None),
        P("tile", None, "seg", None, None),
        P("tile", "seg", None, None),
        P("tile", None, "seg", None, None),
        P("tile", "seg", None, None),
    )
    out_specs = P(("seg", "tile"), None)
    return jax.shard_map(shards, mesh=mesh, in_specs=in_specs, out_specs=out_specs, check_vma=False)
```

profile of v0, /device:TPU:2, one launch (start us, length us, event | category | flops | bytes accessed | tf_op | source)
XLA Modules:
  0.0 225.3 jit_solution(6807326557634860335)
XLA Ops:
  6.5 2.7 %fusion.46 = (f32[1,1,8,128,128]{4,3,2,1,0:T(8,128)S(1)}, f32[1,1,8,128,128]{4,3,2,1,0:T(8,128)}, f32[1,1,8,128,128]{4,3,2,1,0:T(8,128)S(1)}, f32[1,1,8,128,128]{4,3,2,1,0:T(8,128)}) fusion(f32[1,4,8,128,128]{4,3,2,1,0:T(8,128)} %param.8), kind=kLoop, calls=%fused_computation.35 | loop fusion | bytes 4194304 | tf_op jit(solution)/shard_map/slice | solution.py:17
  9.9 1.7 reshape_squeeze.16
  11.6 4.5 %fusion.43 = f32[16,64,512]{2,1,0:T(8,128)S(1)} fusion(f32[16,128,512]{2,1,0:T(8,128)} %bitcast.129, f32[1,16,64,128]{3,2,1,0:T(8,128)} %param.7), kind=kOutput, calls=%fused_computation.32 | convolution fusion | flops 805306368 | bytes 6815744 | tf_op jit(solution)/shard_map/nkl,nlr->nkr/dot_general | solution.py:26
  16.1 2.1 fusion.38
  18.2 2.1 fusion.12
  20.4 2.6 %reshape_squeeze.17 = f32[2,4,2,64,2,64]{5,4,3,2,1,0:T(2,128)} reshape(f32[1,1,8,128,128]{4,3,2,1,0:T(8,128)} %get-tuple-element.12) | data formatting | bytes 1048576 | tf_op jit(solution)/shard_map/reshape;squeeze | solution.py:17
  23.0 3.2 %fusion.15 = f32[2,2,4,64,512]{4,3,1,2,0:T(8,128)S(1)} fusion(f32[2,2,4,64,512,1]{4,3,2,1,0,5:T(8,128)S(1)} %bitcast.122, f32[2,4,2,64,2,64]{5,4,3,2,1,0:T(2,128)} %reshape_squeeze.17), kind=kOutput, calls=%fused_computation.13 | convolution fusion | flops 805306368 | bytes 4718592 | tf_op jit(solution)/shard_map/aeuvwx,awexr->auevr/dot_general | solution.py:19
  26.5 1.6 reshape.70
  28.0 3.2 %fusion.18 = f32[1,2,8,64,512]{4,3,1,2,0:T(8,128)S(1)} fusion(f32[2,8,64,512,1]{3,2,1,0,4:T(8,128)S(1)} %bitcast.120, f32[8,2,64,2,64]{4,3,2,1,0:T(2,128)} %reshape.70), kind=kOutput, calls=%fused_computation.14 | convolution fusion | flops 805306368 | bytes 4718592 | tf_op jit(solution)/shard_map/aeuvwx,awexr->auevr/dot_general | solution.py:19
  32.3 3.5 %convolution_bitcast_fusion = f32[16,64,512]{2,1,0:T(8,128)} fusion(f32[16,64,512]{2,1,0:T(8,128)S(1)} %bitcast.127, f32[1,16,64,64]{3,2,1,0:T(8,128)S(1)} %copy-done.4), kind=kOutput, calls=%fused_computation.18 | convolution fusion | flops 402653184 | bytes 4456448 | tf_op jit(solution)/shard_map/nkj,njr->nkr/dot_general | solution.py:33
  35.9 5.8 %all-to-all-start = ((f32[16,64,512]{2,1,0:T(8,128)}), f32[16,64,512]{2,1,0:T(8,128)S(1)}, u32[]{:S(2)}, u32[]{:S(2)}) async-start(f32[16,64,512]{2,1,0:T(8,128)} %convolution_bitcast_fusion), calls=%async_computation | async-start | bytes 4194304 | tf_op jit(solution)/shard_map/all_to_all | solution.py:34
  41.7 2.7 %fusion.45 = (f32[1,1,8,128,128]{4,3,2,1,0:T(8,128)S(1)}, f32[1,1,8,128,128]{4,3,2,1,0:T(8,128)}, f32[1,1,8,128,128]{4,3,2,1,0:T(8,128)}, f32[1,1,8,128,128]{4,3,2,1,0:T(8,128)}) fusion(f32[1,4,8,128,128]{4,3,2,1,0:T(8,128)} %param.10), kind=kLoop, calls=%fused_computation.34 | loop fusion | bytes 4194304 | tf_op jit(solution)/shard_map/slice | solution.py:17
  44.4 2.6 %reshape.73 = f32[8,2,64,2,64]{4,3,2,1,0:T(2,128)} reshape(f32[1,1,8,128,128]{4,3,2,1,0:T(8,128)} %get-tuple-element.7) | data formatting | bytes 1048576 | tf_op jit(solution)/shard_map/reshape.23
  47.1 2.6 %reshape_squeeze.18 = f32[4,2,2,64,2,64]{5,4,3,2,1,0:T(2,128)} reshape(f32[1,1,8,128,128]{4,3,2,1,0:T(8,128)} %get-tuple-element.6) | data formatting | bytes 1048576 | tf_op jit(solution)/shard_map/reshape;squeeze | solution.py:17
  49.7 2.6 %reshape_squeeze.19 = f32[2,4,2,64,2,64]{5,4,3,2,1,0:T(2,128)} reshape(f32[1,1,8,128,128]{4,3,2,1,0:T(8,128)} %get-tuple-element.8) | data formatting | bytes 1048576 | tf_op jit(solution)/shard_map/reshape;squeeze | solution.py:17
  52.3 1.6 reshape.75
  53.9 16.2 %all-to-all-done = f32[16,64,512]{2,1,0:T(8,128)S(1)} async-done(((f32[16,64,512]{2,1,0:T(8,128)}), f32[16,64,512]{2,1,0:T(8,128)S(1)}, u32[]{:S(2)}, u32[]{:S(2)}) %all-to-all-start) | async-done | bytes 2097184 | tf_op jit(solution)/shard_map/all_to_all | solution.py:34
  70.2 3.3 %fusion.33 = f32[8,512,2,64,1]{1,3,4,2,0:T(8,128)S(1)} fusion(f32[8,2,64,512,1]{3,2,1,4,0:T(8,128)S(1)} %bitcast.119, f32[8,2,64,2,64]{4,3,2,1,0:T(2,128)} %reshape.73), kind=kOutput, calls=%fused_computation.22 | convolution fusion | flops 805306368 | bytes 4718592 | tf_op jit(solution)/shard_map/aeuvwx,awexr->auevr/dot_general | solution.py:19
  73.5 2.0 fusion.21
  75.8 1.0 copy-done.2
  76.8 2.0 fusion.24
  80.1 2.0 fusion.27
  82.3 5.1 %fusion.40 = f32[16,512,128]{1,2,0:T(8,128)} fusion(f32[16,64,512]{2,1,0:T(8,128)S(1)} %bitcast.128, f32[1,16,128,64]{2,3,1,0:T(8,128)S(1)} %copy-done), kind=kOutput, calls=%fused_computation.29 | convolution fusion | flops 805306368 | bytes 6815744 | tf_op jit(solution)/shard_map/nlk,nkr->nlr/dot_general | solution.py:39
  87.4 131.0 %reduce-scatter.2.cloned.1.call-done = f32[64,512]{1,0:T(8,128)} async-done(((f32[2048,512]{1,0:T(8,128)}), f32[64,512]{1,0:T(8,128)}) %reduce-scatter.2.cloned.1.call-update) | async-done | bytes 131088 | tf_op jit(solution)/shard_map/reduce_scatter | solution.py:41
  (18 shorter events, 3.7 us)
Async XLA Ops:
  6.5 75.8 %copy-start = (f32[1,16,128,64]{2,3,1,0:T(8,128)S(1)}, f32[1,16,128,64]{2,3,1,0:T(8,128)}, u32[]{:S(2)}) copy-start(f32[1,16,128,64]{2,3,1,0:T(8,128)} %param.11) | copy-start | bytes 1572868
  31.3 1.0 copy-start.4
  35.9 34.3 %all-to-all-start = ((f32[16,64,512]{2,1,0:T(8,128)}), f32[16,64,512]{2,1,0:T(8,128)S(1)}, u32[]{:S(2)}, u32[]{:S(2)}) async-start(f32[16,64,512]{2,1,0:T(8,128)} %convolution_bitcast_fusion), calls=%async_computation | async-start | bytes 4194304 | tf_op jit(solution)/shard_map/all_to_all | solution.py:34
  41.7 176.7 %reduce-scatter.2.cloned.1.call-start = ((), (), s32[]{:S(2)}) async-start(), calls=%async_computation.2 | async-start | bytes 4325376 | tf_op jit(solution)/shard_map/reduce_scatter | solution.py:41
  70.2 3.3 %copy-start.3 = (f32[4,2,2,64,2,64]{5,4,3,2,1,0:T(2,128)S(1)}, f32[4,2,2,64,2,64]{5,4,3,2,1,0:T(2,128)}, u32[]{:S(2)}) copy-start(f32[4,2,2,64,2,64]{5,4,3,2,1,0:T(2,128)} %reshape_squeeze.18) | copy-start | bytes 1572868
  75.6 1.2 copy-start.2
  78.8 1.2 copy-start.1
Sparse Core Ops, SparseCore 0:
  87.5 130.8 reduce-scatter.1
where the time goes:
time: 226 us; the launch traced here: 225 us
  waiting for transfers between devices  147 us (65%)
  matrix products  33.2 us (15%)
  local copies, waits for them, and re-layouts  25.4 us (11%)
  between operations  13.6 us (6%)
  starting transfers between devices  5.84 us (3%)
    reduce_scatter x1, waiting for transfers between devices, tile_product(): return lax.psum_scatter(rows, 'tile', scatter_dimension=0, tiled=True)  131 us
    dot_general x8, matrix products, levels(): jnp.einsum('aeuvwx,awexr->auevr', wide, split, precision=lax.Precision.HI...  20 us
    all_to_all x1, waiting for transfers between devices, tile_product(): lax.all_to_all(coeffs, 'seg', split_axis=0, concat_axis=0, tiled=True)  16.2 us
    another operation x4, local copies, waits for them, and re-layouts, levels(): wide = weights[level].reshape(blocks, stride, 2, K, 2, K)  9.53 us
    another operation x4, local copies, waits for them, and re-layouts  6.42 us
    all_to_all x1, starting transfers between devices, tile_product(): lax.all_to_all(coeffs, 'seg', split_axis=0, concat_axis=0, tiled=True)  5.84 us
    slice x2, local copies, waits for them, and re-layouts, levels(): wide = weights[level].reshape(blocks, stride, 2, K, 2, K)  5.45 us
    dot_general x1, matrix products, tile_product(): jnp.einsum('nlk,nkr->nlr', expand, coeffs, precision=lax.Precision.HIGHEST)  5.05 us
  transfers between devices with their start and end apart: 2, of which 2 were waited for; matrix products, arithmetic and copies ran while one was open for 5% of the time, Pallas kernels for 0%

commit v1 on v0

v1 whole, which is shorter than its diff:
```python
import functools

import jax
import jax.numpy as jnp
from jax import lax
from jax.experimental import pallas as pl
from jax.experimental.pallas import tpu as pltpu
from jax.sharding import PartitionSpec as P

K = 64
LEAF = 128
BOX = 16
R = 512
C = 4
W = R // C
ROWS = BOX * LEAF
F32 = jnp.float32
BF16 = jnp.bfloat16
MESH = pl.DeviceIdType.MESH
PEERS = ((2, 1), (1, 1), (3, 1), (2, 0), (1, 0), (3, 0), (0, 1))


def halves(v):
    hi = v.astype(BF16)
    return hi, (v - hi.astype(F32)).astype(BF16)


def wide(v):
    return jnp.concatenate(halves(v), axis=1)


def product(weight, hl):
    r = jnp.dot(weight, jnp.concatenate([hl, hl], axis=0), preferred_element_type=F32)
    n = r.shape[1] // 2
    return r[:, :n] + r[:, n:]


def exact(a, b):
    hl = wide(b)
    ahi, alo = halves(a)
    r = jnp.dot(ahi, hl, preferred_element_type=F32) + jnp.dot(alo, hl, preferred_element_type=F32)
    n = r.shape[1] // 2
    return r[:, :n] + r[:, n:]


def level(l, weights, src, dst):
    d = 2**l
    for a in range(BOX // (2 * d)):
        for e in range(d):
            p, j = a * 2 * d + e, a * d + e
            y = product(weights[j], jnp.concatenate([src[p], src[p + d]], axis=0))
            dst[p] = wide(y[:K])
            dst[p + d] = wide(y[K:])


def kernel(
    x_hbm, proj_hbm, col_hbm, mid_hbm, row_hbm, exp_hbm, out,
    xbuf, proj, col, mid, row, expt,
    wproj, wcol, wrow, wend, hla, hlb,
    coef, got, own, pair, rp, rm, fin, ysend, yrecv,
    lsem, asend, arecv, csem, dsend, drecv, psend, precv, msend, mrecv, ysems, yrecvs,
):
    tile, seg = lax.axis_index("tile"), lax.axis_index("seg")
    core, z, yh = tile % 2, (tile // 2) % 8, tile // 16
    xx, yl = seg // 2, seg % 2

    def at(core=core, z=z, yh=yh, xx=xx, yl=yl):
        return ((yh * 8 + z) * 2 + core, xx * 2 + yl)

    other = at(core=1 - core)
    zup, zdown = at(z=(z + 1) % 8), at(z=(z + 7) % 8)
    far = at(yh=1 - yh)
    peers = [at(xx=(xx + dx) % 4, yl=(yl + dy) % 2) for dx, dy in PEERS]

    barrier = pltpu.get_barrier_semaphore()
    friends = peers + [other, zup, zdown, far]
    for f in friends:
        pl.semaphore_signal(barrier, inc=1, device_id=f, device_id_type=MESH)

    def xcopy(c):
        lanes = pl.ds(pl.multiple_of(c * W, W), W)
        return pltpu.make_async_copy(x_hbm.at[:, lanes], xbuf.at[c], lsem.at[c])

    loads = [
        pltpu.make_async_copy(src.at[0], dst, lsem.at[C + i])
        for i, (src, dst) in enumerate(
            ((proj_hbm, proj), (col_hbm, col), (mid_hbm, mid), (row_hbm, row), (exp_hbm, expt))
        )
    ]
    loads[0].start()
    xcopy(0).start()
    loads[1].start()
    loads[2].start()
    for c in range(1, C):
        xcopy(c).start()
    loads[3].start()
    loads[4].start()

    def remote(src, dst, send, recv, to):
        return pltpu.make_async_remote_copy(
            src_ref=src, dst_ref=dst, send_sem=send, recv_sem=recv, device_id=to, device_id_type=MESH
        )

    def spread(c, k):
        to = peers[k]
        return remote(coef.at[c, to[1]], got.at[c, seg], asend.at[c, k], arecv.at[c, k], to)

    def keep(c):
        return pltpu.make_async_copy(coef.at[c, seg], got.at[c, seg], csem.at[c])

    def swap(c):
        return remote(own.at[c, 1 - core], pair.at[c], dsend.at[c], drecv.at[c], other)

    def up(c, src, slot):
        return remote(src, rp.at[c, slot], psend.at[c, slot], precv.at[c, slot], zup)

    def down(c, src, slot):
        return remote(src, rm.at[c, slot], msend.at[c, slot], mrecv.at[c, slot], zdown)

    def cross(c):
        return remote(ysend.at[c], yrecv.at[c], ysems.at[c], yrecvs.at[c], far)

    loads[0].wait()
    for n in range(BOX):
        wproj[n] = wide(proj[n])
    loads[1].wait()

    @pl.loop(0, 3)
    def _(l):
        for j in range(8):
            wcol[l, j] = wide(col[l, j])

    loads[2].wait()
    for j in range(8):
        wcol[3, j, :K] = wide(exact(mid[j], col[3, j, :K]))
        wcol[3, j, K:] = wide(exact(mid[j + 8], col[3, j, K:]))

    @pl.loop(0, C)
    def _(c):
        xcopy(c).wait()
        for n in range(BOX):
            hla[n] = wide(product(wproj[n], wide(xbuf[c, n * LEAF : (n + 1) * LEAF])))
        level(0, wcol.at[0], hla, hlb)
        level(1, wcol.at[1], hlb, hla)
        level(2, wcol.at[2], hla, hlb)
        for j in range(8):
            y = product(wcol[3, j], jnp.concatenate([hlb[j], hlb[j + 8]], axis=0))
            rows = slice((j % 2) * K, (j % 2) * K + K)
            coef[c, j // 2, rows] = y[:K]
            coef[c, j // 2 + 4, rows] = y[K:]

        @pl.when(c == 0)
        def _():
            pl.semaphore_wait(barrier, len(friends))

        for k in range(len(PEERS)):
            spread(c, k).start()
        keep(c).start()

    loads[3].wait()

    @pl.loop(0, 3)
    def _(l):
        for j in range(8):
            wrow[l, j] = wide(row[l, j])

    loads[4].wait()
    for j in range(8):
        wend[j, :LEAF] = wide(exact(expt[j].T, row[3, j, :K]))
        wend[j, LEAF:] = wide(exact(expt[j + 8].T, row[3, j, K:]))

    def begin(c):
        swap(c).wait_recv()
        for jj in (4, 3, 5, 2, 6, 1, 7, 0):
            zz = (z + jj) % 8
            for b in range(2):
                n = b * 8 + zz
                own[c, core, n] = own[c, core, n] + pair[c, n]
            if jj == 4:
                up(c, own.at[c, core, zz], 0).start()
                down(c, own.at[c, core, 8 + zz], 0).start()
            if jj == 3:
                up(c, own.at[c, core, 8 + zz], 2).start()
            if jj == 5:
                down(c, own.at[c, core, zz], 2).start()

    def chain(c, j):
        for e in range(1 if j == 3 else 2):
            here = {3: 0, 2: 1, 1: 3}[j] + e
            there = {3: 1, 2: 3, 1: 5}[j] + e
            up(c, rp.at[c, here], here).wait_recv()
            rp[c, here] = rp[c, here] + own[c, core, e * 8 + (z + j) % 8]
            up(c, rp.at[c, here], there).start()
            down(c, rm.at[c, here], here).wait_recv()
            rm[c, here] = rm[c, here] + own[c, core, (1 - e) * 8 + (z + 8 - j) % 8]
            down(c, rm.at[c, here], there).start()

    def arrive(c):
        for e in range(2):
            up(c, rp.at[c, 5 + e], 5 + e).wait_recv()
            down(c, rm.at[c, 5 + e], 5 + e).wait_recv()

        def total(b):
            return own[c, core, b * 8 + z] + rp[c, 5 + b] + rm[c, 6 - b]

        ysend[c] = total(1 - yh)
        cross(c).start()
        fin[c] = total(yh)

    def finish(c):
        cross(c).wait_recv()
        out[:, pl.ds(pl.multiple_of(c * W, W), W)] = fin[c] + yrecv[c]

    @pl.loop(0, C)
    def _(c):
        for k in range(len(PEERS)):
            spread(c, k).wait_recv()
        keep(c).wait()
        for g in range(8):
            y = product(wrow[0, g], wide(got[c, g]))
            hla[2 * g] = wide(y[:K])
            hla[2 * g + 1] = wide(y[K:])
        level(1, wrow.at[1], hla, hlb)
        level(2, wrow.at[2], hlb, hla)
        for j in range(8):
            y = product(wend[j], jnp.concatenate([hla[j], hla[j + 8]], axis=0))
            for half in range(2):
                for m in range(2):
                    r0 = half * LEAF + m * K
                    own[c, m, half * 8 + j] = y[r0 : r0 + K]
        swap(c).start()

        @pl.when(c >= 1)
        def _():
            chain(c - 1, 2)

        @pl.when(c >= 2)
        def _():
            arrive(c - 2)

        begin(c)

        @pl.when(c >= 1)
        def _():
            chain(c - 1, 1)

        @pl.when(c >= 2)
        def _():
            finish(c - 2)

        chain(c, 3)

    chain(C - 1, 2)
    arrive(C - 2)
    chain(C - 1, 1)
    finish(C - 2)
    arrive(C - 1)
    finish(C - 1)

    @pl.loop(0, C)
    def _(c):
        for k in range(len(PEERS)):
            spread(c, k).wait_send()
        swap(c).wait_send()
        for slot in range(7):
            up(c, rp.at[c, slot], slot).wait_send()
            down(c, rm.at[c, slot], slot).wait_send()
        cross(c).wait_send()


def shards(right_sides, leaf_proj, col_levels, middle_factor, row_levels, leaf_expand):
    dma = pltpu.SemaphoreType.DMA
    vmem = pltpu.VMEM
    return pl.pallas_call(
        kernel,
        out_shape=jax.ShapeDtypeStruct((K, R), F32),
        in_specs=[pl.BlockSpec(memory_space=pl.ANY)] * 6,
        out_specs=pl.BlockSpec(memory_space=pltpu.VMEM),
        scratch_shapes=[
            vmem((C, ROWS, W), F32),
            vmem((BOX, K, LEAF), F32),
            vmem((4, 8, LEAF, LEAF), F32),
            vmem((BOX, K, K), F32),
            vmem((4, 8, LEAF, LEAF), F32),
            vmem((BOX, K, LEAF), F32),
            vmem((BOX, K, 2 * LEAF), BF16),
            vmem((4, 8, LEAF, 2 * LEAF), BF16),
            vmem((3, 8, LEAF, 2 * LEAF), BF16),
            vmem((8, 2 * LEAF, 2 * LEAF), BF16),
            vmem((BOX, K, 2 * W), BF16),
            vmem((BOX, K, 2 * W), BF16),
            vmem((C, 8, LEAF, W), F32),
            vmem((C, 8, LEAF, W), F32),
            vmem((C, 2, BOX, K, W), F32),
            vmem((C, BOX, K, W), F32),
            vmem((C, 7, K, W), F32),
            vmem((C, 7, K, W), F32),
            vmem((C, K, W), F32),
            vmem((C, K, W), F32),
            vmem((C, K, W), F32),
            dma((C + 5,)),
            dma((C, 7)),
            dma((C, 7)),
            dma((C,)),
            dma((C,)),
            dma((C,)),
            dma((C, 7)),
            dma((C, 7)),
            dma((C, 7)),
            dma((C, 7)),
            dma((C,)),
            dma((C,)),
        ],
        compiler_params=pltpu.CompilerParams(
            collective_id=0, has_side_effects=True, vmem_limit_bytes=60 * 1024 * 1024
        ),
        name="butterfly",
    )(right_sides, leaf_proj, col_levels, middle_factor, row_levels, jnp.swapaxes(leaf_expand, 2, 3))


def solution(mesh):
    in_specs = (
        P(("tile", "seg"), None),
        P("tile", "seg", None, None),
        P("tile", None, "seg", None, None),
        P("tile", "seg", None, None),
        P("tile", None, "seg", None, None),
        P("tile", "seg", None, None),
    )
    out_specs = P(("seg", "tile"), None)
    return jax.shard_map(shards, mesh=mesh, in_specs=in_specs, out_specs=out_specs, check_vma=False)
```

time: 226 us -> 68.6 us (0.30)
  waiting for transfers between devices: 147 us -> 0 us
  Pallas kernels: 0 us -> 66.9 us
  matrix products: 33.2 us -> 0 us
  local copies, waits for them, and re-layouts: 25.4 us -> 1.57 us
  between operations: 13.6 us -> 0.01 us
  starting transfers between devices: 5.84 us -> 0 us
    reduce_scatter x1 -> x0, waiting for transfers between devices: 131 us -> none  [tile_product(): return lax.psum_scatter(rows, 'tile', scatter_dimension=0, tiled=True)]
    pallas_call x0 -> x1, Pallas kernels: none -> 66.9 us  [shards(): pl.pallas_call(kernel, out_shape=jax.ShapeDtypeStruct((K, R), F32), in_sp...]
    dot_general x11 -> x0, matrix products: 33.2 us -> none  [the longest x8 20 us: levels(): jnp.einsum('aeuvwx,awexr->auevr', wide, split, precision=lax.Precision.HI...]
    all_to_all x1 -> x0, waiting for transfers between devices: 16.2 us -> none  [tile_product(): lax.all_to_all(coeffs, 'seg', split_axis=0, concat_axis=0, tiled=True)]
    another operation x8 -> x0, local copies, waits for them, and re-layouts: 16 us -> none  [the longest x4 9.53 us: levels(): wide = weights[level].reshape(blocks, stride, 2, K, 2, K)]
    all_to_all x1 -> x0, starting transfers between devices: 5.84 us -> none  [tile_product(): lax.all_to_all(coeffs, 'seg', split_axis=0, concat_axis=0, tiled=True)]
    slice x2 -> x0, local copies, waits for them, and re-layouts: 5.45 us -> none  [levels(): wide = weights[level].reshape(blocks, stride, 2, K, 2, K)]
  transfers between devices with their start and end apart: 2 -> 0, of which waited for: 2 -> 0; matrix products, arithmetic and copies ran while one was open for 5% -> 0% of each run, Pallas kernels for 0% -> 0%
where the time goes in v1:
time: 68.6 us; the launch traced here: 68.5 us
  Pallas kernels  66.9 us (98%)
  local copies, waits for them, and re-layouts  1.57 us (2%)
    pallas_call x1, Pallas kernels, shards(): pl.pallas_call(kernel, out_shape=jax.ShapeDtypeStruct((K, R), F32), in_sp...  66.9 us
    unnamed x1, local copies, waits for them, and re-layouts  1.57 us

profile of v1, /device:TPU:2, one launch (start us, length us, event | category | flops | bytes accessed | tf_op | source)
XLA Modules:
  0.0 68.5 jit_solution(5626351604000661234)
XLA Ops:
  0.0 66.9 %butterfly.1 = f32[64,512]{1,0:T(8,128)} custom-call(f32[2048,512]{1,0:T(8,128)} %x_hbm.1, f32[1,16,64,128]{3,2,1,0:T(8,128)} %proj_hbm.1, f32[1,4,8,128,128]{4,3,2,1,0:T(8,128)} %col_hbm.1, f32[1,16,64,64]{3,2,1,0:T(8,128)} %mid_hbm.1, f32[1,4,8,128,128]{4,3,2,1,0:T(8,128)} %row_hbm.1, f32[1,16,64,128]{3,2,1,0:T(8,128)} %bitcast.1), custom_call_target="tpu_custom_call" | custom-call | tf_op jit(solution)/shard_map/butterfly/pallas_call | solution.py:274
  66.9 1.6 %copy.8 = f32[64,512]{1,0:T(8,128)} copy(f32[64,512]{1,0:T(8,128)} %butterfly.1) | data formatting | bytes 262144

commit v2 on v1

v2 whole, which is shorter than its diff:
```python
import functools

import jax
import jax.numpy as jnp
from jax import lax
from jax.experimental import pallas as pl
from jax.experimental.pallas import tpu as pltpu
from jax.sharding import PartitionSpec as P

K = 64
LEAF = 128
BOX = 16
R = 512
C = 4
W = R // C
ROWS = BOX * LEAF
F32 = jnp.float32
BF16 = jnp.bfloat16
MESH = pl.DeviceIdType.MESH
PEERS = ((2, 1), (1, 1), (3, 1), (2, 0), (1, 0), (3, 0), (0, 1))

LATE = 2
TURN = (4, 3, 5, 2, 6, 1, 7, 0)
FIRST = (4, 5)
ORDER = (
    "R0", "B0", "R1", "M0", "B1", "N0", "R2", "M1",
    "A0", "B2", "N1", "F0", "R3", "B3", "M2", "A1",
    "M3", "F1", "F2", "F3",
)


def halves(v):
    hi = v.astype(BF16)
    return hi, (v - hi.astype(F32)).astype(BF16)


def wide(v):
    return jnp.concatenate(halves(v), axis=1)


def product(weight, hl):
    r = jnp.dot(weight, jnp.concatenate([hl, hl], axis=0), preferred_element_type=F32)
    n = r.shape[1] // 2
    return r[:, :n] + r[:, n:]


def exact(a, b):
    hl = wide(b)
    ahi, alo = halves(a)
    r = jnp.dot(ahi, hl, preferred_element_type=F32) + jnp.dot(alo, hl, preferred_element_type=F32)
    n = r.shape[1] // 2
    return r[:, :n] + r[:, n:]


def level(l, weights, src, dst):
    d = 2**l
    for a in range(BOX // (2 * d)):
        for e in range(d):
            p, j = a * 2 * d + e, a * d + e
            y = product(weights[j], jnp.concatenate([src[p], src[p + d]], axis=0))
            dst[p] = wide(y[:K])
            dst[p + d] = wide(y[K:])


def kernel(
    x_hbm, proj_hbm, col_hbm, mid_hbm, row_hbm, exp_hbm, out,
    xbuf, proj, col, mid, row, expt,
    wproj, wcol, wrow, wend, hla, hlb,
    coef, got, own, pair, rp, rm, fin, ysend, yrecv, ends,
    lsem, asend, arecv, csem, dsend, drecv, psend, precv, msend, mrecv, ysems, yrecvs, esend, erecv,
):
    tile, seg = lax.axis_index("tile"), lax.axis_index("seg")
    core, z, yh = tile % 2, (tile // 2) % 8, tile // 16
    xx, yl = seg // 2, seg % 2

    def at(core=core, z=z, yh=yh, xx=xx, yl=yl):
        return ((yh * 8 + z) * 2 + core, xx * 2 + yl)

    other = at(core=1 - core)
    along = {k: at(z=(z + 8 + k) % 8) for k in (1, 2, -1, -2)}
    aside = [at(yh=1 - yh, z=(z + 8 + k) % 8) for k in (1, 2, -1, -2)]
    far = at(yh=1 - yh)
    peers = [at(xx=(xx + dx) % 4, yl=(yl + dy) % 2) for dx, dy in PEERS]

    barrier = pltpu.get_barrier_semaphore()
    friends = peers + [other, far] + list(along.values()) + aside
    for f in friends:
        pl.semaphore_signal(barrier, inc=1, device_id=f, device_id_type=MESH)

    def xcopy(c):
        lanes = pl.ds(pl.multiple_of(c * W, W), W)
        return pltpu.make_async_copy(x_hbm.at[:, lanes], xbuf.at[c], lsem.at[c])

    loads = [
        pltpu.make_async_copy(src, dst, lsem.at[C + i])
        for i, (src, dst) in enumerate(
            [(proj_hbm.at[0], proj), (mid_hbm.at[0], mid), (row_hbm.at[0], row), (exp_hbm.at[0], expt)]
            + [(col_hbm.at[0, l], col.at[l]) for l in range(4)]
        )
    ]
    loads[0].start()
    xcopy(0).start()
    for l in range(4):
        loads[4 + l].start()
    loads[1].start()
    for c in range(1, C):
        xcopy(c).start()
    loads[2].start()
    loads[3].start()

    def remote(src, dst, send, recv, to):
        return pltpu.make_async_remote_copy(
            src_ref=src, dst_ref=dst, send_sem=send, recv_sem=recv, device_id=to, device_id_type=MESH
        )

    def spread(c, k):
        to = peers[k]
        return remote(coef.at[c, to[1]], got.at[c, seg], asend.at[c, k], arecv.at[c, k], to)

    def keep(c):
        return pltpu.make_async_copy(coef.at[c, seg], got.at[c, seg], csem.at[c])

    def swap(c, j):
        two = pl.ds(j * 2, 2)
        return remote(own.at[c, 1 - core, two], pair.at[c, two], dsend.at[c, j], drecv.at[c, j], other)

    def ring(way, c, src, slot, hops=1):
        if way > 0:
            return remote(src, rp.at[c, slot], psend.at[c, slot], precv.at[c, slot], along[hops])
        return remote(src, rm.at[c, slot], msend.at[c, slot], mrecv.at[c, slot], along[-hops])

    def final(c, kind, way, e, src, who=None):
        w = 0 if way > 0 else 1
        who = yh if who is None else who
        b = e if way > 0 else 1 - e
        return remote(
            src, ends.at[c - LATE, kind, w, who], esend.at[c - LATE, kind, w, e], erecv.at[c - LATE, kind, w, who],
            at(yh=b, z=(z + 8 + way * (1 + kind)) % 8),
        )

    def direct(c):
        return remote(own.at[c, core, z * 2 + 1 - yh], yrecv.at[c], ysems.at[c], yrecvs.at[c], far)

    def held(way):
        return rp if way > 0 else rm

    def landed(way, c, slot):
        ring(way, c, held(way).at[c, slot], slot).wait_recv()

    def mine(way, e, off):
        return (z + 8 + way * off) % 8 * 2 + (e if way > 0 else 1 - e)

    def cross(c):
        return remote(ysend.at[c], yrecv.at[c], ysems.at[c], yrecvs.at[c], far)

    def project(c):
        for n in range(BOX):
            hla[n] = wide(product(wproj[n], wide(xbuf[c, n * LEAF : (n + 1) * LEAF])))

    def last(c):
        for j in range(8):
            y = product(wcol[3, j], jnp.concatenate([hlb[j], hlb[j + 8]], axis=0))
            rows = slice((j % 2) * K, (j % 2) * K + K)
            coef[c, j // 2, rows] = y[:K]
            coef[c, j // 2 + 4, rows] = y[K:]

    def send(c):
        for k in range(len(PEERS)):
            spread(c, k).start()

    ping = ((hla, hlb), (hlb, hla), (hla, hlb))
    loads[0].wait()
    for n in range(BOX):
        wproj[n] = wide(proj[n])
    xcopy(0).wait()
    project(0)
    for l in range(3):
        loads[4 + l].wait()
        for j in range(8):
            wcol[l, j] = wide(col[l, j])
        level(l, wcol.at[l], *ping[l])
    loads[7].wait()
    loads[1].wait()
    for j in range(8):
        wcol[3, j, :K] = wide(exact(mid[j], col[3, j, :K]))
        wcol[3, j, K:] = wide(exact(mid[j + 8], col[3, j, K:]))
    last(0)
    pl.semaphore_wait(barrier, len(friends))
    send(0)
    keep(0).start()

    @pl.loop(1, C)
    def _(c):
        xcopy(c).wait()
        project(c)
        for l in range(3):
            level(l, wcol.at[l], *ping[l])
        last(c)
        keep(c).start()

    loads[2].wait()

    @pl.loop(0, 3)
    def _(l):
        for j in range(8):
            wrow[l, j] = wide(row[l, j])

    loads[3].wait()
    for j in range(8):
        wend[j, :LEAF] = wide(exact(expt[j].T, row[3, j, :K]))
        wend[j, LEAF:] = wide(exact(expt[j + 8].T, row[3, j, K:]))

    def begin(c):
        for jj in TURN:
            zz = (z + jj) % 8
            swap(c, zz).wait_recv()
            for b in range(2):
                own[c, core, zz * 2 + b] = own[c, core, zz * 2 + b] + pair[c, zz * 2 + b]
            if jj == 4:
                for way in (1, -1):
                    ring(way, c, own.at[c, core, mine(way, 0, 4)], 0, 2).start()
            if jj in (3, 5):
                way = 4 - jj
                for e in range(2):
                    ring(way, c, own.at[c, core, mine(way, e, 3)], 1 + e).start()
            if c >= LATE and jj in (1, 7):
                way = 1 if jj == 1 else -1
                for e in range(2):
                    final(c, 0, way, e, own.at[c, core, mine(way, e, 1)]).start()
            if c >= LATE and jj == 0:
                direct(c).start()

    def middle(c):
        for e in range(2):
            for way in (1, -1):
                buf = held(way)
                part = own[c, core, mine(way, e, 2)]
                if e == 0:
                    landed(way, c, 0)
                    part = part + buf[c, 0]
                landed(way, c, 1 + e)
                buf[c, 1 + e] = buf[c, 1 + e] + part
                if c >= LATE:
                    final(c, 1, way, e, buf.at[c, 1 + e]).start()
                else:
                    ring(way, c, buf.at[c, 1 + e], 3 + e).start()

    def near(c):
        for e in range(2):
            for way in (1, -1):
                buf = held(way)
                landed(way, c, 3 + e)
                buf[c, 3 + e] = buf[c, 3 + e] + own[c, core, mine(way, e, 1)]
                ring(way, c, buf.at[c, 3 + e], 5 + e).start()

    def arrive(c):
        for e in range(2):
            for way in (1, -1):
                landed(way, c, 5 + e)

        def total(b):
            return own[c, core, z * 2 + b] + rp[c, 5 + b] + rm[c, 6 - b]

        ysend[c] = total(1 - yh)
        cross(c).start()
        fin[c] = total(yh)

    def finish(c):
        if c >= LATE:
            t = own[c, core, z * 2 + yh]
            for kind in range(2):
                for way in (0, 1):
                    for who in range(2):
                        final(c, kind, 1 - 2 * way, 0, ysend.at[c], who).wait_recv()
                        t = t + ends[c - LATE, kind, way, who]
            direct(c).wait_recv()
        else:
            cross(c).wait_recv()
            t = fin[c]
        out[:, c * W : (c + 1) * W] = t + yrecv[c]

    def rows(c):
        for k in FIRST:
            spread(c, k).wait_recv()
        if c + 1 < C:
            send(c + 1)
        for k in range(len(PEERS)):
            if k not in FIRST:
                spread(c, k).wait_recv()
        keep(c).wait()
        for g in range(8):
            y = product(wrow[0, g], wide(got[c, g]))
            hla[2 * g] = wide(y[:K])
            hla[2 * g + 1] = wide(y[K:])
        level(1, wrow.at[1], hla, hlb)
        level(2, wrow.at[2], hlb, hla)
        for jj in TURN:
            j = (z + jj) % 8
            y = product(wend[j], jnp.concatenate([hla[j], hla[j + 8]], axis=0))
            for half in range(2):
                for m in range(2):
                    r0 = half * LEAF + m * K
                    own[c, m, j * 2 + half] = y[r0 : r0 + K]
            swap(c, j).start()

    steps = {
        "R": rows,
        "B": begin,
        "M": middle,
        "N": near,
        "A": arrive,
        "F": finish,
    }
    for step in ORDER:
        steps[step[0]](int(step[1:]))

    @pl.loop(0, C)
    def _(c):
        for k in range(len(PEERS)):
            spread(c, k).wait_send()
        for j in range(8):
            swap(c, j).wait_send()
        for way in (1, -1):
            for slot in range(3):
                ring(way, c, held(way).at[c, slot], slot).wait_send()
        cross(c).wait_send()

    @pl.loop(0, LATE)
    def _(c):
        for way in (1, -1):
            for slot in range(3, 7):
                ring(way, c, held(way).at[c, slot], slot).wait_send()

    @pl.loop(LATE, C)
    def _(c):
        for kind in range(2):
            for way in (1, -1):
                for e in range(2):
                    final(c, kind, way, e, ysend.at[c]).wait_send()


def shards(right_sides, leaf_proj, col_levels, middle_factor, row_levels, leaf_expand):
    dma = pltpu.SemaphoreType.DMA
    vmem = pltpu.VMEM
    return pl.pallas_call(
        kernel,
        out_shape=jax.ShapeDtypeStruct((K, R), F32),
        in_specs=[pl.BlockSpec(memory_space=pl.ANY)] * 6,
        out_specs=pl.BlockSpec(memory_space=pltpu.VMEM),
        scratch_shapes=[
            vmem((C, ROWS, W), F32),
            vmem((BOX, K, LEAF), F32),
            vmem((4, 8, LEAF, LEAF), F32),
            vmem((BOX, K, K), F32),
            vmem((4, 8, LEAF, LEAF), F32),
            vmem((BOX, K, LEAF), F32),
            vmem((BOX, K, 2 * LEAF), BF16),
            vmem((4, 8, LEAF, 2 * LEAF), BF16),
            vmem((3, 8, LEAF, 2 * LEAF), BF16),
            vmem((8, 2 * LEAF, 2 * LEAF), BF16),
            vmem((BOX, K, 2 * W), BF16),
            vmem((BOX, K, 2 * W), BF16),
            vmem((C, 8, LEAF, W), F32),
            vmem((C, 8, LEAF, W), F32),
            vmem((C, 2, BOX, K, W), F32),
            vmem((C, BOX, K, W), F32),
            vmem((C, 7, K, W), F32),
            vmem((C, 7, K, W), F32),
            vmem((C, K, W), F32),
            vmem((C, K, W), F32),
            vmem((C, K, W), F32),
            vmem((C - LATE, 2, 2, 2, K, W), F32),
            dma((C + 8,)),
            dma((C, 7)),
            dma((C, 7)),
            dma((C,)),
            dma((C, 8)),
            dma((C, 8)),
            dma((C, 7)),
            dma((C, 7)),
            dma((C, 7)),
            dma((C, 7)),
            dma((C,)),
            dma((C,)),
            dma((C - LATE, 2, 2, 2)),
            dma((C - LATE, 2, 2, 2)),
        ],
        compiler_params=pltpu.CompilerParams(
            collective_id=0, has_side_effects=True, vmem_limit_bytes=60 * 1024 * 1024
        ),
        name="butterfly",
    )(right_sides, leaf_proj, col_levels, middle_factor, row_levels, jnp.swapaxes(leaf_expand, 2, 3))


def solution(mesh):
    in_specs = (
        P(("tile", "seg"), None),
        P("tile", "seg", None, None),
        P("tile", None, "seg", None, None),
        P("tile", "seg", None, None),
        P("tile", None, "seg", None, None),
        P("tile", "seg", None, None),
    )
    out_specs = P(("seg", "tile"), None)
    return jax.shard_map(shards, mesh=mesh, in_specs=in_specs, out_specs=out_specs, check_vma=False)
```

time: 68.6 us -> 60.1 us (0.88)
  Pallas kernels: 66.9 us -> 58.5 us
    pallas_call x1, Pallas kernels: 66.9 us -> 58.5 us  [shards(): pl.pallas_call(kernel, out_shape=jax.ShapeDtypeStruct((K, R), F32), in_sp...]
where the time goes in v2:
time: 60.1 us
  Pallas kernels  58.5 us (97%)
  local copies, waits for them, and re-layouts  1.57 us (3%)
    pallas_call x1, Pallas kernels, shards(): pl.pallas_call(kernel, out_shape=jax.ShapeDtypeStruct((K, R), F32), in_sp...  58.5 us
    unnamed x1, local copies, waits for them, and re-layouts  1.57 us

profile of v2, /device:TPU:2, one launch (start us, length us, event | category | flops | bytes accessed | tf_op | source)
XLA Modules:
  0.0 60.1 jit_solution(17027535629113250022)
XLA Ops:
  0.0 58.5 %butterfly.1 = f32[64,512]{1,0:T(8,128)} custom-call(f32[2048,512]{1,0:T(8,128)} %x_hbm.1, f32[1,16,64,128]{3,2,1,0:T(8,128)} %proj_hbm.1, f32[1,4,8,128,128]{4,3,2,1,0:T(8,128)} %col_hbm.1, f32[1,16,64,64]{3,2,1,0:T(8,128)} %mid_hbm.1, f32[1,4,8,128,128]{4,3,2,1,0:T(8,128)} %row_hbm.1, f32[1,16,64,128]{3,2,1,0:T(8,128)} %bitcast.1), custom_call_target="tpu_custom_call" | custom-call | tf_op jit(solution)/shard_map/butterfly/pallas_call | solution.py:345
  58.5 1.6 %copy.8 = f32[64,512]{1,0:T(8,128)} copy(f32[64,512]{1,0:T(8,128)} %butterfly.1) | data formatting | bytes 262144

commit v3 on v2

--- a/solution.py
+++ b/solution.py
@@ -21,7 +21,7 @@
 
 LATE = 2
 TURN = (4, 3, 5, 2, 6, 1, 7, 0)
-FIRST = (4, 5)
+FIRST = (4, 5, 6)
 ORDER = (
     "R0", "B0", "R1", "M0", "B1", "N0", "R2", "M1",
     "A0", "B2", "N1", "F0", "R3", "B3", "M2", "A1",

time: 60.1 us -> 62.5 us (1.040)
  the two profiles are of different devices: /device:TPU:2 before, /device:TPU:16 now
where the time goes in v3:
time: 62.5 us; the launch traced here: 62.4 us
  Pallas kernels  60.8 us (97%)
  local copies, waits for them, and re-layouts  1.57 us (3%)
    pallas_call x1, Pallas kernels, shards(): pl.pallas_call(kernel, out_shape=jax.ShapeDtypeStruct((K, R), F32), in_sp...  60.8 us
    unnamed x1, local copies, waits for them, and re-layouts  1.57 us

profile of v3, /device:TPU:16, one launch (start us, length us, event | category | flops | bytes accessed | tf_op | source)
XLA Modules:
  0.0 62.4 jit_solution(557337674314571924)
XLA Ops:
  0.0 60.8 %butterfly.1 = f32[64,512]{1,0:T(8,128)} custom-call(f32[2048,512]{1,0:T(8,128)} %x_hbm.1, f32[1,16,64,128]{3,2,1,0:T(8,128)} %proj_hbm.1, f32[1,4,8,128,128]{4,3,2,1,0:T(8,128)} %col_hbm.1, f32[1,16,64,64]{3,2,1,0:T(8,128)} %mid_hbm.1, f32[1,4,8,128,128]{4,3,2,1,0:T(8,128)} %row_hbm.1, f32[1,16,64,128]{3,2,1,0:T(8,128)} %bitcast.1), custom_call_target="tpu_custom_call" | custom-call | tf_op jit(solution)/shard_map/butterfly/pallas_call | solution.py:345
  60.8 1.6 %copy.8 = f32[64,512]{1,0:T(8,128)} copy(f32[64,512]{1,0:T(8,128)} %butterfly.1) | data formatting | bytes 262144
